TPU v7x, 512 devices: a whole 4x8x8 slice. The times are simulated.
512 devices in a mesh: mp: 16 (over x_lo, y), dp: 32 (over x_hi, z, core).
Axes of the slice: x: 4 (x_hi: 2, x_lo: 2; x = x_hi * 2 + x_lo), y: 8, z: 8, core: 2. Of those that a mesh axis runs over, the one named last changes fastest.
Arguments:
- activations: bfloat16 [16, 2048, 8192], P('mp', 'dp'), may hold values from -54 to 54
- cotangents: bfloat16 [16, 2048, 1792], P('mp', 'dp'), may hold values from -54 to 54
- label_mask: int32 [16, 2048], P('mp', 'dp'), may hold values from 0 to 1, as said below
- checkpoints: bfloat16 [16, 8192, 1792], P('mp', 'dp'), may hold values from -6 to 6
Outputs:
- merged: bfloat16 [8192, 1792], P('dp')
Inputs may be any that keep to these rules, and one draw needn't show every extreme that they name: `label_mask`: the last token of every checkpoint is labelled.
All inputs are finite; a program needn't handle non-finite values.
Results may differ from a plain program's by a relative error of at most 0.0025.
Values may be sent and summed in bfloat16 or wider, within the bound.
A program may use at most 64 MiB of HBM per device.

v0:
```python
import jax
import jax.numpy as jnp
from jax import lax
from jax.sharding import PartitionSpec as P


def contract_tokens(feature_sq, block_cot):
    return lax.dot_general(
        feature_sq, block_cot, (((0,), (0,)), ((), ())), preferred_element_type=jnp.float32
    )


def per_device(activations, cotangents, label_mask, checkpoints):
    tok_acts = activations[0]
    tok_mask = label_mask[0]
    own_slab = checkpoints[0]
    label_weight = tok_mask.astype(jnp.float32)
    cot_square = (label_weight[:, None] * jnp.square(cotangents[0].astype(jnp.float32))).astype(
        jnp.bfloat16
    )
    act_square = jnp.square(tok_acts.astype(jnp.float32)).astype(jnp.bfloat16)
    feature_sq = lax.all_to_all(act_square, "dp", split_axis=1, concat_axis=0, tiled=True)
    fisher_sum = contract_tokens(feature_sq, lax.all_gather(cot_square, "dp", axis=0, tiled=True))
    labelled = lax.psum(jnp.sum(label_weight), "dp")
    fisher = fisher_sum / labelled
    weighted = fisher * own_slab.astype(jnp.float32)
    numerator, denominator = lax.psum((weighted, fisher), "mp")
    merged = (numerator / denominator).astype(jnp.bfloat16)
    return merged


def solution(mesh):
    return jax.shard_map(
        per_device,
        mesh=mesh,
        in_specs=(P("mp", "dp", None), P("mp", "dp", None), P("mp", "dp"), P("mp", "dp", None)),
        out_specs=P("dp", None),
        check_vma=False,
    )
```

profile of v0, /device:TPU:4, one launch (start us, length us, event | category | flops | bytes accessed | tf_op | source)
XLA Modules:
  0.0 296.8 jit_solution(10089826524948816606)
XLA Ops:
  6.5 0.0 all-gather.2.cloned.1.call-start
  6.5 0.7 convert_bitcast_fusion
  7.2 1.7 fusion
  8.9 0.0 all-gather.2.cloned.1.call-update
  8.9 1.4 multiply_convert_fusion
  10.3 0.3 copy.7
  10.6 0.0 copy-start.1
  10.6 0.0 copy-start
  10.6 1.6 copy.6
  12.2 13.4 %all-to-all-start = ((bf16[64,32,256]{2,0,1:T(8,128)(2,1)}), bf16[64,32,256]{2,0,1:T(8,128)(2,1)S(1)}, u32[]{:S(2)}, u32[]{:S(2)}) async-start(bf16[64,32,256]{2,0,1:T(8,128)(2,1)} %copy.6), calls=%async_computation | async-start | bytes 2097152 | tf_op jit(solution)/shard_map/all_to_all | solution.py:22
  25.7 0.0 all-reduce.3.cloned.1.call-start
  25.7 0.0 copy-done.1
  25.7 0.6 convert_reduce_fusion
  26.3 88.2 %psum.21 = f32[]{:T(128)} all-reduce(f32[]{:T(128)} %convert_reduce_fusion), channel_id=1, replica_groups=mesh['mp'=16,'dp'=32] {'dp'}, use_global_device_ids=true, to_apply=%region_1.0 | all-reduce | flops 1 | bytes 8 | tf_op jit(solution)/shard_map/psum | solution.py:24
  114.5 0.0 all-to-all-done
  114.5 9.9 %all-gather.2.cloned.1.call-done = bf16[2048,1792]{1,0:T(8,128)(2,1)} async-done(((bf16[64,1792]{1,0:T(8,128)(2,1)}), bf16[2048,1792]{1,0:T(8,128)(2,1)}) %all-gather.2.cloned.1.call-update) | async-done | bytes 7340048 | tf_op jit(solution)/shard_map/all_gather | solution.py:23
  124.4 0.0 copy-done
  124.4 7.7 %convert_multiply_fusion = (f32[256,1792]{1,0:T(8,128)}, f32[256,1792]{1,0:T(8,128)}) fusion(bf16[1,256,1792]{2,1,0:T(8,128)(2,1)S(1)} %copy-done, f32[]{:T(128)} %psum.21, bf16[2048,256]{1,0:T(8,128)(2,1)S(1)} %bitcast.19, bf16[2048,1792]{1,0:T(8,128)(2,1)} %all-gather.2.cloned.1.call-done), kind=kOutput, calls=%fused_computation.2 | convolution fusion | flops 1880424448 | bytes 12976132 | tf_op jit(solution)/shard_map/dot_general | solution.py:8
  132.1 0.0 all-reduce.3.cloned.1.call-update
  132.1 154.6 %all-reduce.3.cloned.1.call-done = (f32[256,1792]{1,0:T(8,128)}, f32[256,1792]{1,0:T(8,128)}) async-done(((f32[256,1792]{1,0:T(8,128)}, f32[256,1792]{1,0:T(8,128)}), (f32[256,1792]{1,0:T(8,128)}, f32[256,1792]{1,0:T(8,128)})) %all-reduce.3.cloned.1.call-update) | async-done | bytes 3670032 | tf_op jit(solution)/shard_map/psum | solution.py:27
  286.7 3.2 %divide_convert_fusion = bf16[256,1792]{1,0:T(8,128)(2,1)} fusion(f32[256,1792]{1,0:T(8,128)} %get-tuple-element.5, f32[256,1792]{1,0:T(8,128)} %get-tuple-element.6), kind=kLoop, calls=%fused_computation.3 | loop fusion | flops 917504 | bytes 4587520 | tf_op jit(solution)/shard_map/convert_element_type | solution.py:28
Async XLA Ops:
  6.5 117.9 %all-gather.2.cloned.1.call-start = ((), (), s32[]{:S(2)}) async-start(), calls=%async_computation.1 | async-start | bytes 7569408 | tf_op jit(solution)/shard_map/all_gather | solution.py:23
  10.6 15.1 %copy-start.1 = (s32[1,64]{1,0:T(1,128)S(1)}, s32[1,64]{1,0:T(1,128)}, u32[]{:S(2)}) copy-start(s32[1,64]{1,0:T(1,128)} %param.6) | copy-start | bytes 772
  10.6 113.8 %copy-start = (bf16[1,256,1792]{2,1,0:T(8,128)(2,1)S(1)}, bf16[1,256,1792]{2,1,0:T(8,128)(2,1)}, u32[]{:S(2)}) copy-start(bf16[1,256,1792]{2,1,0:T(8,128)(2,1)} %param.7) | copy-start | bytes 2752516
  12.2 102.3 %all-to-all-start = ((bf16[64,32,256]{2,0,1:T(8,128)(2,1)}), bf16[64,32,256]{2,0,1:T(8,128)(2,1)S(1)}, u32[]{:S(2)}, u32[]{:S(2)}) async-start(bf16[64,32,256]{2,0,1:T(8,128)(2,1)} %copy.6), calls=%async_computation | async-start | bytes 2097152 | tf_op jit(solution)/shard_map/all_to_all | solution.py:22
  25.7 261.1 %all-reduce.3.cloned.1.call-start = ((), (), s32[]{:S(2)}) async-start(), calls=%async_computation.2 | async-start | bytes 7340032 | tf_op jit(solution)/shard_map/psum | solution.py:27
Sparse Core Ops, SparseCore 0:
  10.7 113.6 all-gather.1
  132.3 154.4 all-reduce.2
where the time goes:
time: 297 us
  waiting for transfers between devices  165 us (56%)
  blocking collectives  88.2 us (30%)
  starting transfers between devices  13.5 us (5%)
  between operations  13.4 us (5%)
  matrix products  7.7 us (3%)
  other arithmetic  7.61 us (3%)
    psum x1, waiting for transfers between devices, per_device(): numerator, denominator = lax.psum((weighted, fisher), 'mp')  155 us
    psum x1, blocking collectives, per_device(): labelled = lax.psum(jnp.sum(label_weight), 'dp')  88.2 us
    all_to_all x1, starting transfers between devices, per_device(): lax.all_to_all(act_square, 'dp', split_axis=1, concat_axis=0, tiled=True)  13.4 us
    all_gather x1, waiting for transfers between devices, per_device(): lax.all_gather(cot_square, 'dp', axis=0, tiled=True)  9.88 us
    dot_general x1, matrix products, contract_tokens(): lax.dot_general(feature_sq, block_cot, (((0,), (0,)), ((), ())), preferre...  7.7 us
  transfers between devices with their start and end apart: 3, of which 2 were waited for; matrix products, arithmetic and copies ran while one was open for 1% of the time, Pallas kernels for 0%

commit v1 on v0

--- a/solution.py
+++ b/solution.py
@@ -20,7 +20,10 @@
     )
     act_square = jnp.square(tok_acts.astype(jnp.float32)).astype(jnp.bfloat16)
     feature_sq = lax.all_to_all(act_square, "dp", split_axis=1, concat_axis=0, tiled=True)
-    fisher_sum = contract_tokens(feature_sq, lax.all_gather(cot_square, "dp", axis=0, tiled=True))
+    unite_indices_for = lambda xx: jnp.concatenate(
+        lax.all_to_all(jnp.stack(lax.axis_size("dp") * [xx], axis=0), "dp", 0, 0), axis=0
+    )
+    fisher_sum = contract_tokens(feature_sq, unite_indices_for(cot_square))
     labelled = lax.psum(jnp.sum(label_weight), "dp")
     fisher = fisher_sum / labelled
     weighted = fisher * own_slab.astype(jnp.float32)

time: 297 us -> 450 us (1.52)
  blocking collectives: 88.2 us -> 217 us
  waiting for transfers between devices: 165 us -> 180 us
  starting transfers between devices: 13.5 us -> 21.1 us
    psum x1, blocking collectives: 88.2 us -> 217 us  [per_device(): labelled = lax.psum(jnp.sum(label_weight), 'dp')]
    all_to_all x1, waiting for transfers between devices: 0.01 us -> 27.1 us  [per_device(): lax.all_to_all(act_square, 'dp', split_axis=1, concat_axis=0, tiled=True)]
    all_gather x1 -> x0, waiting for transfers between devices: 9.88 us -> none  [per_device(): lax.all_gather(cot_square, 'dp', axis=0, tiled=True)]
    all_to_all x0 -> x1, starting transfers between devices: none -> 7.57 us  [per_device(): lax.all_to_all(jnp.stack(lax.axis_size('dp') * [xx], axis=0), 'dp', 0, 0)]
  transfers between devices with their start and end apart: 3 -> 3, of which waited for: 2 -> 2; matrix products, arithmetic and copies ran while one was open for 1% -> 0% of each run, Pallas kernels for 0% -> 0%
where the time goes in v1:
time: 450 us
  blocking collectives  217 us (48%)
  waiting for transfers between devices  180 us (40%)
  starting transfers between devices  21.1 us (5%)
  between operations  13.5 us (3%)
  matrix products  7.72 us (2%)
  local copies, waits for them, and re-layouts  5.68 us (1%)
  other arithmetic  5.31 us (1%)
    psum x1, blocking collectives, per_device(): labelled = lax.psum(jnp.sum(label_weight), 'dp')  217 us
    psum x1, waiting for transfers between devices, per_device(): numerator, denominator = lax.psum((weighted, fisher), 'mp')  153 us
    all_to_all x1, waiting for transfers between devices, per_device(): lax.all_to_all(act_square, 'dp', split_axis=1, concat_axis=0, tiled=True)  27.1 us
    all_to_all x1, starting transfers between devices, per_device(): lax.all_to_all(act_square, 'dp', split_axis=1, concat_axis=0, tiled=True)  13.4 us
  transfers between devices with their start and end apart: 3, of which 2 were waited for; matrix products, arithmetic and copies ran while one was open for 0% of the time, Pallas kernels for 0%

profile of v1, /device:TPU:4, one launch (start us, length us, event | category | flops | bytes accessed | tf_op | source)
XLA Modules:
  0.0 449.7 jit_solution(17766040786689214350)
XLA Ops:
  6.5 1.4 multiply_convert_fusion
  7.9 0.3 copy.6
  8.2 0.0 copy-start.2
  8.2 0.0 copy-start
  8.2 1.5 copy.5
  9.8 13.4 %all-to-all-start = ((bf16[64,32,256]{2,0,1:T(8,128)(2,1)}), bf16[64,32,256]{2,0,1:T(8,128)(2,1)S(1)}, u32[]{:S(2)}, u32[]{:S(2)}) async-start(bf16[64,32,256]{2,0,1:T(8,128)(2,1)} %copy.5), calls=%async_computation | async-start | bytes 2097152 | tf_op jit(solution)/shard_map/all_to_all | solution.py:22
  23.2 0.0 copy-done.2
  23.2 0.0 copy-done
  23.3 0.1 fusion.2
  23.4 27.1 %all-to-all-done = bf16[64,32,256]{2,0,1:T(8,128)(2,1)S(1)} async-done(((bf16[64,32,256]{2,0,1:T(8,128)(2,1)}), bf16[64,32,256]{2,0,1:T(8,128)(2,1)S(1)}, u32[]{:S(2)}, u32[]{:S(2)}) %all-to-all-start) | async-done | bytes 1048608 | tf_op jit(solution)/shard_map/all_to_all | solution.py:22
  50.5 3.9 stack.5
  54.4 0.0 copy-start.1
  54.4 7.6 %all-to-all-start.1 = ((bf16[32,64,1792]{2,1,0:T(8,128)(2,1)}), bf16[32,64,1792]{2,1,0:T(8,128)(2,1)}, u32[]{:S(2)}, u32[]{:S(2)}) async-start(bf16[32,64,1792]{2,1,0:T(8,128)(2,1)} %stack.5), calls=%async_computation.1 | async-start | bytes 14680064 | tf_op jit(solution)/shard_map/all_to_all | solution.py:24
  61.9 0.0 all-reduce.3.cloned.1.call-start
  62.0 0.6 convert_reduce_fusion
  62.6 216.6 %psum.21 = f32[]{:T(128)} all-reduce(f32[]{:T(128)} %convert_reduce_fusion), channel_id=1, replica_groups=mesh['mp'=16,'dp'=32] {'dp'}, use_global_device_ids=true, to_apply=%region_1.0 | all-reduce | flops 1 | bytes 8 | tf_op jit(solution)/shard_map/psum | solution.py:27
  279.1 0.0 all-to-all-done.1
  279.1 0.0 copy-done.1
  279.1 7.7 %convert_multiply_fusion = (f32[256,1792]{1,0:T(8,128)}, f32[256,1792]{1,0:T(8,128)}) fusion(bf16[1,256,1792]{2,1,0:T(8,128)(2,1)S(1)} %copy-done.1, f32[]{:T(128)} %psum.21, bf16[32,64,1792]{2,1,0:T(8,128)(2,1)} %all-to-all-done.1, bf16[64,32,256]{2,0,1:T(8,128)(2,1)S(1)} %all-to-all-done), kind=kOutput, calls=%fused_computation.3 | convolution fusion | flops 1880424448 | bytes 12976132 | tf_op jit(solution)/shard_map/dot_general | solution.py:8
  286.9 0.0 all-reduce.3.cloned.1.call-update
  286.9 152.8 %all-reduce.3.cloned.1.call-done = (f32[256,1792]{1,0:T(8,128)}, f32[256,1792]{1,0:T(8,128)}) async-done(((f32[256,1792]{1,0:T(8,128)}, f32[256,1792]{1,0:T(8,128)}), (f32[256,1792]{1,0:T(8,128)}, f32[256,1792]{1,0:T(8,128)})) %all-reduce.3.cloned.1.call-update) | async-done | bytes 3670032 | tf_op jit(solution)/shard_map/psum | solution.py:30
  439.6 3.2 divide_convert_fusion
  (1 shorter events, 0.0 us)
Async XLA Ops:
  8.2 15.0 %copy-start.2 = (s32[1,64]{1,0:T(1,128)S(1)}, s32[1,64]{1,0:T(1,128)}, u32[]{:S(2)}) copy-start(s32[1,64]{1,0:T(1,128)} %param.6) | copy-start | bytes 772
  8.2 15.0 %copy-start = (bf16[1,64,1792]{2,1,0:T(8,128)(2,1)S(1)}, bf16[1,64,1792]{2,1,0:T(8,128)(2,1)}, u32[]{:S(2)}) copy-start(bf16[1,64,1792]{2,1,0:T(8,128)(2,1)} %param.5) | copy-start | bytes 688132
  9.8 40.7 %all-to-all-start = ((bf16[64,32,256]{2,0,1:T(8,128)(2,1)}), bf16[64,32,256]{2,0,1:T(8,128)(2,1)S(1)}, u32[]{:S(2)}, u32[]{:S(2)}) async-start(bf16[64,32,256]{2,0,1:T(8,128)(2,1)} %copy.5), calls=%async_computation | async-start | bytes 2097152 | tf_op jit(solution)/shard_map/all_to_all | solution.py:22
  54.4 224.8 %copy-start.1 = (bf16[1,256,1792]{2,1,0:T(8,128)(2,1)S(1)}, bf16[1,256,1792]{2,1,0:T(8,128)(2,1)}, u32[]{:S(2)}) copy-start(bf16[1,256,1792]{2,1,0:T(8,128)(2,1)} %param.7) | copy-start | bytes 2752516
  54.4 224.8 %all-to-all-start.1 = ((bf16[32,64,1792]{2,1,0:T(8,128)(2,1)}), bf16[32,64,1792]{2,1,0:T(8,128)(2,1)}, u32[]{:S(2)}, u32[]{:S(2)}) async-start(bf16[32,64,1792]{2,1,0:T(8,128)(2,1)} %stack.5), calls=%async_computation.1 | async-start | bytes 14680064 | tf_op jit(solution)/shard_map/all_to_all | solution.py:24
  61.9 377.7 %all-reduce.3.cloned.1.call-start = ((), (), s32[]{:S(2)}) async-start(), calls=%async_computation.2 | async-start | bytes 7340032 | tf_op jit(solution)/shard_map/psum | solution.py:30
Sparse Core Ops, SparseCore 0:
  287.0 152.5 all-reduce.2

commit v2 on v0

--- a/solution.py
+++ b/solution.py
@@ -19,7 +19,19 @@
         jnp.bfloat16
     )
     act_square = jnp.square(tok_acts.astype(jnp.float32)).astype(jnp.bfloat16)
-    feature_sq = lax.all_to_all(act_square, "dp", split_axis=1, concat_axis=0, tiled=True)
+
+    def sections_play(buf):
+        return jnp.concatenate(
+            lax.all_to_all(
+                jnp.stack(jnp.split(buf, lax.axis_size("dp"), axis=1)),
+                axis_name="dp",
+                split_axis=0,
+                concat_axis=0,
+            ),
+            axis=0,
+        )
+
+    feature_sq = sections_play(act_square)
     fisher_sum = contract_tokens(feature_sq, lax.all_gather(cot_square, "dp", axis=0, tiled=True))
     labelled = lax.psum(jnp.sum(label_weight), "dp")
     fisher = fisher_sum / labelled

time: 297 us -> 304 us (1.024)
  local copies, waits for them, and re-layouts: 1.85 us -> 19.7 us
  waiting for transfers between devices: 165 us -> 154 us
    unnamed x5 -> x35, local copies, waits for them, and re-layouts: 0.27 us -> 19.1 us
    all_gather x1, waiting for transfers between devices: 9.88 us -> 0.01 us  [per_device(): lax.all_gather(cot_square, 'dp', axis=0, tiled=True)]
  transfers between devices with their start and end apart: 3 -> 3, of which waited for: 2 -> 1; matrix products, arithmetic and copies ran while one was open for 1% -> 7% of each run, Pallas kernels for 0% -> 0%
where the time goes in v2:
time: 304 us; the launch traced here: 303 us
  waiting for transfers between devices  154 us (51%)
  blocking collectives  87.4 us (29%)
  local copies, waits for them, and re-layouts  19.7 us (6%)
  starting transfers between devices  13.5 us (4%)
  between operations  13.4 us (4%)
  matrix products  7.71 us (3%)
  other arithmetic  7.61 us (3%)
    psum x1, waiting for transfers between devices, per_device(): numerator, denominator = lax.psum((weighted, fisher), 'mp')  154 us
    psum x1, blocking collectives, per_device(): labelled = lax.psum(jnp.sum(label_weight), 'dp')  87.4 us
    unnamed x35, local copies, waits for them, and re-layouts  19.1 us
    all_to_all x1, starting transfers between devices, sections_play(): lax.all_to_all(jnp.stack(jnp.split(buf, lax.axis_size('dp'), axis=1)), ax...  13.4 us
    dot_general x1, matrix products, contract_tokens(): lax.dot_general(feature_sq, block_cot, (((0,), (0,)), ((), ())), preferre...  7.71 us
  transfers between devices with their start and end apart: 3, of which 1 were waited for; matrix products, arithmetic and copies ran while one was open for 7% of the time, Pallas kernels for 0%

profile of v2, /device:TPU:4, one launch (start us, length us, event | category | flops | bytes accessed | tf_op | source)
XLA Modules:
  0.0 303.5 jit_solution(4291136958018169059)
XLA Ops:
  6.5 0.0 all-gather.2.cloned.1.call-start
  6.5 0.7 convert_bitcast_fusion
  7.2 1.7 fusion.1
  8.9 0.0 all-gather.2.cloned.1.call-update
  8.9 1.4 fusion
  10.3 0.6 constant_dynamic-update-slice_fusion.31
  11.0 0.6 constant_dynamic-update-slice_fusion.30
  11.6 0.6 constant_dynamic-update-slice_fusion.29
  12.2 0.6 constant_dynamic-update-slice_fusion.28
  12.8 0.6 constant_dynamic-update-slice_fusion.27
  13.4 0.6 constant_dynamic-update-slice_fusion.26
  14.0 0.6 constant_dynamic-update-slice_fusion.25
  14.7 0.6 constant_dynamic-update-slice_fusion.24
  15.3 0.0 copy-start.1
  15.3 0.0 copy-start
  15.3 0.6 constant_dynamic-update-slice_fusion.23
  15.9 0.6 constant_dynamic-update-slice_fusion.22
  16.5 0.6 constant_dynamic-update-slice_fusion.21
  17.1 0.6 constant_dynamic-update-slice_fusion.20
  17.7 0.6 constant_dynamic-update-slice_fusion.19
  18.4 0.6 constant_dynamic-update-slice_fusion.18
  19.0 0.6 constant_dynamic-update-slice_fusion.17
  19.6 0.6 constant_dynamic-update-slice_fusion.16
  20.2 0.6 constant_dynamic-update-slice_fusion.15
  20.8 0.6 constant_dynamic-update-slice_fusion.14
  21.4 0.6 constant_dynamic-update-slice_fusion.13
  22.0 0.6 constant_dynamic-update-slice_fusion.12
  22.7 0.6 constant_dynamic-update-slice_fusion.11
  23.3 0.6 constant_dynamic-update-slice_fusion.10
  23.9 0.6 constant_dynamic-update-slice_fusion.9
  24.5 0.6 constant_dynamic-update-slice_fusion.8
  25.1 0.6 constant_dynamic-update-slice_fusion.7
  25.7 0.6 constant_dynamic-update-slice_fusion.6
  26.4 0.6 constant_dynamic-update-slice_fusion.5
  27.0 0.6 constant_dynamic-update-slice_fusion.4
  27.6 0.6 constant_dynamic-update-slice_fusion.3
  28.2 0.6 constant_dynamic-update-slice_fusion.2
  28.8 0.6 constant_dynamic-update-slice_fusion.1
  29.5 0.6 constant_dynamic-update-slice_fusion
  30.1 13.4 %all-to-all-start = ((bf16[32,64,256]{2,1,0:T(8,128)(2,1)}), bf16[32,64,256]{2,1,0:T(8,128)(2,1)S(1)}, u32[]{:S(2)}, u32[]{:S(2)}) async-start(bf16[32,64,256]{2,1,0:T(8,128)(2,1)} %constant_dynamic-update-slice_fusion), calls=%async_computation | async-start | bytes 2097152 | tf_op jit(solution)/shard_map/all_to_all | solution.py:25
  43.5 0.0 all-reduce.3.cloned.1.call-start
  43.6 0.0 copy-done.1
  43.6 0.6 convert_reduce_fusion
  44.2 87.4 %psum.21 = f32[]{:T(128)} all-reduce(f32[]{:T(128)} %convert_reduce_fusion), channel_id=1, replica_groups=mesh['mp'=16,'dp'=32] {'dp'}, use_global_device_ids=true, to_apply=%region_1.0 | all-reduce | flops 1 | bytes 8 | tf_op jit(solution)/shard_map/psum | solution.py:36
  131.6 0.0 all-to-all-done
  131.6 0.0 all-gather.2.cloned.1.call-done
  131.6 0.0 copy-done
  131.6 7.7 %convert_multiply_fusion = (f32[256,1792]{1,0:T(8,128)}, f32[256,1792]{1,0:T(8,128)}) fusion(bf16[1,256,1792]{2,1,0:T(8,128)(2,1)S(1)} %copy-done, f32[]{:T(128)} %psum.21, bf16[2048,256]{1,0:T(8,128)(2,1)S(1)} %bitcast.142, bf16[2048,1792]{1,0:T(8,128)(2,1)} %all-gather.2.cloned.1.call-done), kind=kOutput, calls=%fused_computation.2 | convolution fusion | flops 1880424448 | bytes 12976132 | tf_op jit(solution)/shard_map/dot_general | solution.py:8
  139.3 0.0 all-reduce.3.cloned.1.call-update
  139.4 154.0 %all-reduce.3.cloned.1.call-done = (f32[256,1792]{1,0:T(8,128)}, f32[256,1792]{1,0:T(8,128)}) async-done(((f32[256,1792]{1,0:T(8,128)}, f32[256,1792]{1,0:T(8,128)}), (f32[256,1792]{1,0:T(8,128)}, f32[256,1792]{1,0:T(8,128)})) %all-reduce.3.cloned.1.call-update) | async-done | bytes 3670032 | tf_op jit(solution)/shard_map/psum | solution.py:39
  293.4 3.2 %divide_convert_fusion = bf16[256,1792]{1,0:T(8,128)(2,1)} fusion(f32[256,1792]{1,0:T(8,128)} %get-tuple-element.5, f32[256,1792]{1,0:T(8,128)} %get-tuple-element.6), kind=kLoop, calls=%fused_computation.3 | loop fusion | flops 917504 | bytes 4587520 | tf_op jit(solution)/shard_map/convert_element_type | solution.py:40
Async XLA Ops:
  6.5 125.1 %all-gather.2.cloned.1.call-start = ((), (), s32[]{:S(2)}) async-start(), calls=%async_computation.1 | async-start | bytes 7569408 | tf_op jit(solution)/shard_map/all_gather | solution.py:35
  15.3 28.3 %copy-start.1 = (s32[1,64]{1,0:T(1,128)S(1)}, s32[1,64]{1,0:T(1,128)}, u32[]{:S(2)}) copy-start(s32[1,64]{1,0:T(1,128)} %param.6) | copy-start | bytes 772
  15.3 116.4 %copy-start = (bf16[1,256,1792]{2,1,0:T(8,128)(2,1)S(1)}, bf16[1,256,1792]{2,1,0:T(8,128)(2,1)}, u32[]{:S(2)}) copy-start(bf16[1,256,1792]{2,1,0:T(8,128)(2,1)} %param.7) | copy-start | bytes 2752516
  30.1 101.6 %all-to-all-start = ((bf16[32,64,256]{2,1,0:T(8,128)(2,1)}), bf16[32,64,256]{2,1,0:T(8,128)(2,1)S(1)}, u32[]{:S(2)}, u32[]{:S(2)}) async-start(bf16[32,64,256]{2,1,0:T(8,128)(2,1)} %constant_dynamic-update-slice_fusion), calls=%async_computation | async-start | bytes 2097152 | tf_op jit(solution)/shard_map/all_to_all | solution.py:25
  43.5 249.9 %all-reduce.3.cloned.1.call-start = ((), (), s32[]{:S(2)}) async-start(), calls=%async_computation.2 | async-start | bytes 7340032 | tf_op jit(solution)/shard_map/psum | solution.py:39
Sparse Core Ops, SparseCore 0:
  10.7 112.3 all-gather.1
  139.5 153.8 all-reduce.2
